TPU v7x, 32 devices: a whole 2x2x4 slice. The times are simulated.
32 devices in a mesh: aux: 4 (over x, core), cd: 4 (over z), ab: 2 (over y).
Axes of the slice: x: 2, y: 2, z: 4, core: 2. Of those that a mesh axis runs over, the one named last changes fastest.
Arguments:
- left_integrals: bfloat16 [4, 2048, 2048], P('cd', 'ab', 'aux'), may hold values from -6 to 6
- right_integrals: bfloat16 [2, 2048, 2048], P('ab', 'cd', 'aux'), may hold values from -6 to 6
- metric_factor: bfloat16 [2048, 2048], P('aux'), may hold values from -0.125 to 0.125
- amplitudes: bfloat16 [32, 2048, 2048], P(None, 'ab', 'cd'), may hold values from -6.4373016e-05 to 6.4373016e-05
- tile_sizes: int32 [16], replicated, may hold values from 1 to 256, 2048 in all
- pair_mask: int32 [16, 16], replicated, may hold values 0 or 1
Outputs:
- ladder_residual: float32 [4, 2, 32], P('cd', 'ab')
Inputs may be any that keep to these rules, and one draw needn't show every extreme that they name: `tile_sizes`: the 16 tile sizes sum to 2048.
All inputs are finite; a program needn't handle non-finite values.
Results may differ from a plain program's by a relative error of at most 0.0038.
Values may be sent and summed in bfloat16 or wider, within the bound.
A program may use at most 128 MiB of HBM per device.

v0:
```python
import jax
import jax.numpy as jnp
from jax import lax
from jax.sharding import PartitionSpec as P


def region_keep(tile_sizes, pair_mask, c_offset, c_count, d_offset, d_count):
    tile_end = jnp.cumsum(tile_sizes)
    tile_range = jnp.arange(tile_end.shape[0], dtype=jnp.int32)

    def onehot(offset, count):
        positions = offset + jnp.arange(count, dtype=jnp.int32)
        tile_index = jnp.sum((positions[:, None] >= tile_end[None, :]).astype(jnp.int32), axis=1)
        return (tile_index[:, None] == tile_range[None, :]).astype(jnp.float32)

    left_hot = onehot(c_offset, c_count)
    right_hot = onehot(d_offset, d_count)
    mask_table = pair_mask.astype(jnp.float32)
    inner = jnp.dot(left_hot, mask_table, precision=lax.Precision.HIGHEST)
    return jnp.dot(inner, right_hot.T, precision=lax.Precision.HIGHEST)


def ladder_terms(left_piece, right_all, kept):
    aux_count = left_piece.shape[0]
    b_count = right_all.shape[1]
    d_width = right_all.shape[2]
    right_flat = right_all.reshape(aux_count, b_count * d_width)

    def one_virtual(left_slab):
        ladder = lax.dot_general(
            left_slab, right_flat, (((0,), (0,)), ((), ())), preferred_element_type=jnp.float32
        )
        ladder = ladder.astype(jnp.bfloat16).reshape(-1, b_count, d_width)
        total = lax.dot_general(
            ladder, kept, (((0, 2), (1, 2)), ((), ())), preferred_element_type=jnp.float32
        )
        return total

    return lax.map(one_virtual, jnp.moveaxis(left_piece, 1, 0))


def body(left_integrals, right_integrals, metric_factor, amplitudes, tile_sizes, pair_mask):
    aux_local = metric_factor.shape[0]
    aux_total = metric_factor.shape[1]
    a_local = left_integrals.shape[0]
    b_local = right_integrals.shape[0]
    c_width = amplitudes.shape[1]
    d_width = amplitudes.shape[2]
    pair_count = amplitudes.shape[0]
    c_offset = lax.axis_index("ab") * c_width
    d_offset = lax.axis_index("cd") * d_width
    left_count = a_local * c_width
    stacked = jnp.concatenate(
        [left_integrals.reshape(-1, aux_local), right_integrals.reshape(-1, aux_local)], axis=0
    )
    share = aux_total // lax.axis_size("aux")
    fitted = lax.psum_scatter(
        lax.dot_general(
            metric_factor, stacked, (((0,), (1,)), ((), ())), preferred_element_type=jnp.float32
        ),
        "aux",
        scatter_dimension=0,
        tiled=True,
    ).astype(jnp.bfloat16)
    left_fit = fitted[:, :left_count].reshape(share, a_local, c_width)
    right_fit = fitted[:, left_count:].reshape(share, b_local, d_width)
    right_all = lax.all_gather(right_fit, "ab", axis=1, tiled=True)
    keep_mask = region_keep(tile_sizes, pair_mask, c_offset, c_width, d_offset, d_width)
    kept = amplitudes * keep_mask.astype(jnp.bfloat16)[None]
    partial_sums = ladder_terms(lax.all_gather(left_fit, "cd", axis=1, tiled=True), right_all, kept)
    flat_terms = partial_sums.reshape(-1, pair_count)
    owned = lax.psum_scatter(flat_terms, ("cd", "ab"), scatter_dimension=0, tiled=True)
    totals = lax.psum(owned, "aux")
    return totals.reshape(a_local, b_local, pair_count)


def solution(mesh):
    return jax.shard_map(
        body,
        mesh=mesh,
        in_specs=(
            P("cd", "ab", "aux"),
            P("ab", "cd", "aux"),
            P("aux", None),
            P(None, "ab", "cd"),
            P(),
            P(),
        ),
        out_specs=P("cd", "ab", None),
        check_vma=False,
    )
```

profile of v0, /device:TPU:0, one launch (start us, length us, event | category | flops | bytes accessed | tf_op | source)
XLA Modules:
  0.0 353.8 jit_solution(16906253457313340899)
XLA Ops:
  6.5 0.0 copy-start
  6.5 0.0 reduce-scatter.2.cloned.1.call-start
  6.5 1.6 copy-done
  8.1 7.8 %convolution_bitcast_fusion.1 = f32[2048,1536]{0,1:T(8,128)} fusion(bf16[512,2048]{1,0:T(8,128)(2,1)S(1)} %copy-done, bf16[512,512]{1,0:T(8,128)(2,1)} %bitcast.43, bf16[1024,512]{1,0:T(8,128)(2,1)} %bitcast.42), kind=kOutput, calls=%fused_computation.7 | convolution fusion | flops 3224371200 | bytes 16252928 | tf_op jit(solution)/shard_map/dot_general | solution.py:58
  15.9 0.0 reduce-scatter.2.cloned.1.call-update
  15.9 0.0 all-gather.7.cloned.1.call-start
  16.0 100.0 %reduce-scatter.2.cloned.1.call-done = f32[512,1536]{0,1:T(8,128)} async-done(((f32[2048,1536]{0,1:T(8,128)}), f32[512,1536]{0,1:T(8,128)}) %reduce-scatter.2.cloned.1.call-update) | async-done | bytes 3145744 | tf_op jit(solution)/shard_map/reduce_scatter | solution.py:57
  116.0 2.1 convert_element_type.20
  118.1 0.0 copy-start.2
  118.1 0.0 copy-start.4
  118.1 0.0 copy-start.3
  118.1 0.9 slice.9
  118.9 0.0 all-gather.7.cloned.1.call-update
  119.0 0.0 all-gather.5.cloned.1.call-start
  119.0 1.0 slice.8
  120.0 0.0 all-gather.5.cloned.1.call-update
  120.1 0.0 copy-done.2
  120.1 0.1 copy.24
  120.2 0.1 reduce
  120.3 0.0 copy-done.4
  120.4 0.6 dynamic-slice
  120.9 0.1 convert_reduce_fusion.1
  121.0 0.1 convert_reduce_fusion
  121.1 0.0 copy-done.3
  121.1 0.5 fusion.7
  121.6 1.1 convolution_convert_fusion.1
  122.7 29.4 %copy_multiply_fusion = bf16[32,1024,512]{2,0,1:T(8,128)(2,1)} fusion(bf16[32,1024,512]{2,1,0:T(8,128)(2,1)} %param.11, bf16[1024,512]{1,0:T(8,128)(2,1)S(1)} %convolution_convert_fusion.1), kind=kLoop, calls=%fused_computation.6 | loop fusion | flops 16777216 | bytes 68157440 | tf_op jit(solution)/shard_map/mul | solution.py:69
  152.1 0.0 all-gather.7.cloned.1.call-done
  152.1 1.5 copy.26
  153.6 69.1 %all-gather.5.cloned.1.call-done = bf16[512,4096]{0,1:T(8,128)(2,1)} async-done(((bf16[512,1024]{0,1:T(8,128)(2,1)}), bf16[512,4096]{0,1:T(8,128)(2,1)}) %all-gather.5.cloned.1.call-update) | async-done | bytes 4194320 | tf_op jit(solution)/shard_map/all_gather | solution.py:70
  222.8 6.3 %copy.23 = bf16[512,4,1024]{2,0,1:T(8,128)(2,1)} copy(bf16[512,4,1024]{0,2,1:T(8,128)(2,1)} %bitcast.38) | data formatting | bytes 8388608 | tf_op jit(solution)/shard_map/all_gather | solution.py:70
  229.1 92.4 %while.10 = (s32[]{:T(128)}, f32[4,2,32]{2,1,0:T(2,128)S(1)}, bf16[4,512,1024]{2,1,0:T(8,128)(2,1)}, bf16[512,1024]{1,0:T(8,128)(2,1)S(1)}, bf16[32,1024,512]{2,0,1:T(8,128)(2,1)}, /*index=5*/s32[]{:T(128)}) while((s32[]{:T(128)}, f32[4,2,32]{2,1,0:T(2,128)S(1)}, bf16[4,512,1024]{2,1,0:T(8,128)(2,1)}, bf16[512,1024]{1,0:T(8,128)(2,1)S(1)}, ...), condition=%wide.region_5.6_spmd, body=%wide.region_4.5_spmd.sunk | while | flops 1141899264 | bytes 44041300 | solution.py:39
  229.1 3.8 %convolution_convert_fusion.3 = bf16[1024,1024]{0,1:T(8,128)(2,1)} fusion(bf16[512,1024]{1,0:T(8,128)(2,1)S(1)} %get-tuple-element.109, bf16[4,512,1024]{2,1,0:T(8,128)(2,1)} %get-tuple-element.108, s32[]{:T(128)S(6)} %copy.33), kind=kOutput, calls=%fused_computation.clone.1 | convolution fusion | flops 1074790400 | bytes 4194308 | tf_op jit(solution)/shard_map/while/body/eval_jaxpr/dot_general | solution.py:30
  232.9 4.8 %copy.29 = bf16[1024,2,512]{2,1,0:T(2,128)(2,1)S(1)} copy(bf16[1024,2,512]{0,2,1:T(8,128)(2,1)} %bitcast.37) | data formatting | bytes 4194304 | tf_op jit(solution)/shard_map/while/body/eval_jaxpr/reshape | solution.py:33
  237.8 14.4 %fusion.26 = f32[4,2,32]{2,1,0:T(2,128)S(1)} fusion(f32[4,2,32]{2,1,0:T(2,128)S(1)} %get-tuple-element.101, s32[]{:T(128)S(6)} %copy.33, bf16[1024,2,512]{2,1,0:T(2,128)(2,1)S(1)} %copy.29, bf16[32,1024,512]{2,0,1:T(8,128)(2,1)} %get-tuple-element.110), kind=kOutput, calls=%fused_computation.2.clone.1 | convolution fusion | flops 67108864 | bytes 35652612 | tf_op jit(solution)/shard_map/while/body/eval_jaxpr/dot_general | solution.py:34
  252.2 3.9 %convolution_convert_fusion.3 = bf16[1024,1024]{0,1:T(8,128)(2,1)} fusion(bf16[512,1024]{1,0:T(8,128)(2,1)S(1)} %get-tuple-element.109, bf16[4,512,1024]{2,1,0:T(8,128)(2,1)} %get-tuple-element.108, s32[]{:T(128)S(6)} %copy.33), kind=kOutput, calls=%fused_computation.clone.1 | convolution fusion | flops 1074790400 | bytes 4194308 | tf_op jit(solution)/shard_map/while/body/eval_jaxpr/dot_general | solution.py:30
  256.1 4.8 %copy.29 = bf16[1024,2,512]{2,1,0:T(2,128)(2,1)S(1)} copy(bf16[1024,2,512]{0,2,1:T(8,128)(2,1)} %bitcast.37) | data formatting | bytes 4194304 | tf_op jit(solution)/shard_map/while/body/eval_jaxpr/reshape | solution.py:33
  260.9 14.4 %fusion.26 = f32[4,2,32]{2,1,0:T(2,128)S(1)} fusion(f32[4,2,32]{2,1,0:T(2,128)S(1)} %get-tuple-element.101, s32[]{:T(128)S(6)} %copy.33, bf16[1024,2,512]{2,1,0:T(2,128)(2,1)S(1)} %copy.29, bf16[32,1024,512]{2,0,1:T(8,128)(2,1)} %get-tuple-element.110), kind=kOutput, calls=%fused_computation.2.clone.1 | convolution fusion | flops 67108864 | bytes 35652612 | tf_op jit(solution)/shard_map/while/body/eval_jaxpr/dot_general | solution.py:34
  275.3 3.9 %convolution_convert_fusion.3 = bf16[1024,1024]{0,1:T(8,128)(2,1)} fusion(bf16[512,1024]{1,0:T(8,128)(2,1)S(1)} %get-tuple-element.109, bf16[4,512,1024]{2,1,0:T(8,128)(2,1)} %get-tuple-element.108, s32[]{:T(128)S(6)} %copy.33), kind=kOutput, calls=%fused_computation.clone.1 | convolution fusion | flops 1074790400 | bytes 4194308 | tf_op jit(solution)/shard_map/while/body/eval_jaxpr/dot_general | solution.py:30
  279.2 4.8 %copy.29 = bf16[1024,2,512]{2,1,0:T(2,128)(2,1)S(1)} copy(bf16[1024,2,512]{0,2,1:T(8,128)(2,1)} %bitcast.37) | data formatting | bytes 4194304 | tf_op jit(solution)/shard_map/while/body/eval_jaxpr/reshape | solution.py:33
  284.0 14.4 %fusion.26 = f32[4,2,32]{2,1,0:T(2,128)S(1)} fusion(f32[4,2,32]{2,1,0:T(2,128)S(1)} %get-tuple-element.101, s32[]{:T(128)S(6)} %copy.33, bf16[1024,2,512]{2,1,0:T(2,128)(2,1)S(1)} %copy.29, bf16[32,1024,512]{2,0,1:T(8,128)(2,1)} %get-tuple-element.110), kind=kOutput, calls=%fused_computation.2.clone.1 | convolution fusion | flops 67108864 | bytes 35652612 | tf_op jit(solution)/shard_map/while/body/eval_jaxpr/dot_general | solution.py:34
  298.4 3.9 %convolution_convert_fusion.3 = bf16[1024,1024]{0,1:T(8,128)(2,1)} fusion(bf16[512,1024]{1,0:T(8,128)(2,1)S(1)} %get-tuple-element.109, bf16[4,512,1024]{2,1,0:T(8,128)(2,1)} %get-tuple-element.108, s32[]{:T(128)S(6)} %copy.33), kind=kOutput, calls=%fused_computation.clone.1 | convolution fusion | flops 1074790400 | bytes 4194308 | tf_op jit(solution)/shard_map/while/body/eval_jaxpr/dot_general | solution.py:30
  302.3 4.8 %copy.29 = bf16[1024,2,512]{2,1,0:T(2,128)(2,1)S(1)} copy(bf16[1024,2,512]{0,2,1:T(8,128)(2,1)} %bitcast.37) | data formatting | bytes 4194304 | tf_op jit(solution)/shard_map/while/body/eval_jaxpr/reshape | solution.py:33
  307.1 14.4 %fusion.26 = f32[4,2,32]{2,1,0:T(2,128)S(1)} fusion(f32[4,2,32]{2,1,0:T(2,128)S(1)} %get-tuple-element.101, s32[]{:T(128)S(6)} %copy.33, bf16[1024,2,512]{2,1,0:T(2,128)(2,1)S(1)} %copy.29, bf16[32,1024,512]{2,0,1:T(8,128)(2,1)} %get-tuple-element.110), kind=kOutput, calls=%fused_computation.2.clone.1 | convolution fusion | flops 67108864 | bytes 35652612 | tf_op jit(solution)/shard_map/while/body/eval_jaxpr/dot_general | solution.py:34
  321.6 19.0 %all-reduce = f32[8,32]{1,0:T(8,128)S(1)} all-reduce(f32[8,32]{1,0:T(8,128)S(1)} %bitcast.40), channel_id=5, replica_groups=mesh['aux'=4,'cd'=4,'ab'=2] {'cd','ab'}, use_global_device_ids=true, to_apply=%region_6.7.clone | all-reduce | flops 256 | bytes 2048
  340.5 0.6 dynamic-slice_bitcast_fusion
  341.1 6.2 %psum.7 = f32[1,1,32]{2,1,0:T(1,128)} all-reduce(f32[1,1,32]{2,1,0:T(1,128)S(1)} %dynamic-slice_bitcast_fusion), channel_id=1, replica_groups=mesh['aux'=4,'cd'=4,'ab'=2] {'aux'}, use_global_device_ids=true, to_apply=%region_7.8 | all-reduce | flops 32 | bytes 256 | tf_op jit(solution)/shard_map/psum | solution.py:73
  347.2 0.0 copy-done.1
  (5 shorter events, 0.0 us)
Async XLA Ops:
  6.5 1.6 copy-start
  6.5 109.4 %reduce-scatter.2.cloned.1.call-start = ((), (), s32[]{:S(2)}) async-start(), calls=%async_computation.1 | async-start | bytes 15728640 | tf_op jit(solution)/shard_map/reduce_scatter | solution.py:57
  15.9 136.2 %all-gather.7.cloned.1.call-start = ((), (), s32[]{:S(2)}) async-start(), calls=%async_computation.3 | async-start | bytes 1572864 | tf_op jit(solution)/shard_map/all_gather | solution.py:67
  118.1 2.0 copy-start.2
  118.1 2.3 copy-start.4
  118.1 3.0 copy-start.3
  119.0 103.8 %all-gather.5.cloned.1.call-start = ((), (), s32[]{:S(2)}) async-start(), calls=%async_computation.2 | async-start | bytes 5242880 | tf_op jit(solution)/shard_map/all_gather | solution.py:70
  321.6 25.7 %copy-start.1 = (bf16[512,2048]{1,0:T(8,128)(2,1)S(1)}, bf16[512,2048]{1,0:T(8,128)(2,1)}, u32[]{:S(2)}) copy-start(bf16[512,2048]{1,0:T(8,128)(2,1)} %param.10) | copy-start | bytes 6291460
Sparse Core Ops, SparseCore 0:
  16.1 99.8 reduce-scatter.1
  119.1 21.2 all-gather.6
  142.0 80.7 all-gather.4
where the time goes:
time: 355 us; the launch traced here: 354 us
  waiting for transfers between devices  169 us (48%)
  matrix products  82.5 us (23%)
  local copies, waits for them, and re-layouts  31.8 us (9%)
  other arithmetic  31.8 us (9%)
  blocking collectives  25.1 us (7%)
  between operations  13.2 us (4%)
    reduce_scatter x1, waiting for transfers between devices, body(): lax.psum_scatter(lax.dot_general(metric_factor, stacked, (((0,), (1,)), (...  100 us
    all_gather x1, waiting for transfers between devices, body(): lax.all_gather(left_fit, 'cd', axis=1, tiled=True)  69.1 us
    dot_general x4, matrix products, one_virtual(): lax.dot_general(ladder, kept, (((0, 2), (1, 2)), ((), ())), preferred_ele...  57.7 us
    mul x1, other arithmetic, body(): kept = amplitudes * keep_mask.astype(jnp.bfloat16)[None]  29.4 us
    reshape x4, local copies, waits for them, and re-layouts, one_virtual(): ladder = ladder.astype(jnp.bfloat16).reshape(-1, b_count, d_width)  19.3 us
    unnamed x1, blocking collectives  19 us
    dot_general x4, matrix products, one_virtual(): lax.dot_general(left_slab, right_flat, (((0,), (0,)), ((), ())), preferre...  15.4 us
    dot_general x1, matrix products, body(): lax.dot_general(metric_factor, stacked, (((0,), (1,)), ((), ())), preferr...  7.79 us
  transfers between devices with their start and end apart: 3, of which 2 were waited for; matrix products, arithmetic and copies ran while one was open for 10% of the time, Pallas kernels for 0%

commit v1 on v0

--- a/solution.py
+++ b/solution.py
@@ -1,7 +1,37 @@
+import functools
 import jax
 import jax.numpy as jnp
 from jax import lax
 from jax.sharding import PartitionSpec as P
+
+
+def _try_all_streams(original, shard_axis, ndim_at):
+    new = lax.axis_size(shard_axis)
+    far_arr = lax.axis_index(shard_axis)
+    prior, spare, vec_out = (new, far_arr, original.shape[ndim_at])
+    big = jnp.zeros(
+        [u * prior if i == ndim_at else u for i, u in enumerate(original.shape)], original.dtype
+    )
+    extra = lax.dynamic_update_slice_in_dim(big, original, spare * vec_out, axis=ndim_at)
+    a_next = met_up = original
+    for at in range(1, prior // 2 + 1):
+        a_next = lax.ppermute(
+            a_next, axis_name=shard_axis, perm=[(i, (i + 1) % prior) for i in range(prior)]
+        )
+        extra = lax.dynamic_update_slice_in_dim(
+            extra, a_next, (spare - at) % prior * vec_out, axis=ndim_at
+        )
+        if 2 * at < prior:
+            met_up = lax.ppermute(
+                met_up, axis_name=shard_axis, perm=[(i, (i - 1) % prior) for i in range(prior)]
+            )
+            extra = lax.dynamic_update_slice_in_dim(
+                extra, met_up, (spare + at) % prior * vec_out, axis=ndim_at
+            )
+    return extra
+
+
+watch_the_clusters = functools.partial(_try_all_streams, shard_axis="cd", ndim_at=1)
 
 
 def region_keep(tile_sizes, pair_mask, c_offset, c_count, d_offset, d_count):
@@ -67,7 +97,7 @@
     right_all = lax.all_gather(right_fit, "ab", axis=1, tiled=True)
     keep_mask = region_keep(tile_sizes, pair_mask, c_offset, c_width, d_offset, d_width)
     kept = amplitudes * keep_mask.astype(jnp.bfloat16)[None]
-    partial_sums = ladder_terms(lax.all_gather(left_fit, "cd", axis=1, tiled=True), right_all, kept)
+    partial_sums = ladder_terms(watch_the_clusters(left_fit), right_all, kept)
     flat_terms = partial_sums.reshape(-1, pair_count)
     owned = lax.psum_scatter(flat_terms, ("cd", "ab"), scatter_dimension=0, tiled=True)
     totals = lax.psum(owned, "aux")

time: 355 us -> 321 us (0.904)
  waiting for transfers between devices: 169 us -> 123 us
  local copies, waits for them, and re-layouts: 31.8 us -> 38.4 us
  starting transfers between devices: 0.09 us -> 3.92 us
    all_gather x1 -> x0, waiting for transfers between devices: 69.1 us -> none  [body(): lax.all_gather(left_fit, 'cd', axis=1, tiled=True)]
    ppermute x0 -> x3, waiting for transfers between devices: none -> 23.2 us  [the longest x2 23.2 us: _try_all_streams(): lax.ppermute(a_next, axis_name=shard_axis, perm=[(i, (i + 1) % prior) for...]
    all_gather x1 -> x0, local copies, waits for them, and re-layouts: 6.35 us -> none  [body(): lax.all_gather(left_fit, 'cd', axis=1, tiled=True)]
    ppermute x0 -> x3, local copies, waits for them, and re-layouts: none -> 4.45 us  [the longest x2 2.96 us: _try_all_streams(): lax.ppermute(a_next, axis_name=shard_axis, perm=[(i, (i + 1) % prior) for...]
    dynamic_update_slice x0 -> x4, local copies, waits for them, and re-layouts: none -> 4.27 us  [the longest x2 2.14 us: _try_all_streams(): lax.dynamic_update_slice_in_dim(extra, a_next, (spare - at) % prior * vec...]
    ppermute x0 -> x3, starting transfers between devices: none -> 3.88 us  [the longest x1 2.39 us: _try_all_streams(): lax.ppermute(met_up, axis_name=shard_axis, perm=[(i, (i - 1) % prior) for...]
  transfers between devices with their start and end apart: 3 -> 5, of which waited for: 2 -> 3; matrix products, arithmetic and copies ran while one was open for 10% -> 14% of each run, Pallas kernels for 0% -> 0%
where the time goes in v1:
time: 321 us; the launch traced here: 320 us
  waiting for transfers between devices  123 us (38%)
  matrix products  82.5 us (26%)
  local copies, waits for them, and re-layouts  38.4 us (12%)
  other arithmetic  31.8 us (10%)
  blocking collectives  26.6 us (8%)
  between operations  13.5 us (4%)
  starting transfers between devices  3.92 us (1%)
    reduce_scatter x1, waiting for transfers between devices, body(): lax.psum_scatter(lax.dot_general(metric_factor, stacked, (((0,), (1,)), (...  100 us
    dot_general x4, matrix products, one_virtual(): lax.dot_general(ladder, kept, (((0, 2), (1, 2)), ((), ())), preferred_ele...  57.7 us
    mul x1, other arithmetic, body(): kept = amplitudes * keep_mask.astype(jnp.bfloat16)[None]  29.4 us
    ppermute x2, waiting for transfers between devices, _try_all_streams(): lax.ppermute(a_next, axis_name=shard_axis, perm=[(i, (i + 1) % prior) for...  23.2 us
    unnamed x1, blocking collectives  20.2 us
    reshape x4, local copies, waits for them, and re-layouts, one_virtual(): ladder = ladder.astype(jnp.bfloat16).reshape(-1, b_count, d_width)  19.3 us
    dot_general x4, matrix products, one_virtual(): lax.dot_general(left_slab, right_flat, (((0,), (0,)), ((), ())), preferre...  15.3 us
    dot_general x1, matrix products, body(): lax.dot_general(metric_factor, stacked, (((0,), (1,)), ((), ())), preferr...  7.79 us
  transfers between devices with their start and end apart: 5, of which 3 were waited for; matrix products, arithmetic and copies ran while one was open for 14% of the time, Pallas kernels for 0%

profile of v1, /device:TPU:0, one launch (start us, length us, event | category | flops | bytes accessed | tf_op | source)
XLA Modules:
  0.0 320.0 jit_solution(627002419919514737)
XLA Ops:
  6.5 1.6 copy-done
  8.1 7.8 %convolution_bitcast_fusion.1 = f32[2048,1536]{0,1:T(8,128)} fusion(bf16[512,2048]{1,0:T(8,128)(2,1)S(1)} %copy-done, bf16[512,512]{1,0:T(8,128)(2,1)} %bitcast.42, bf16[1024,512]{1,0:T(8,128)(2,1)} %bitcast.41), kind=kOutput, calls=%fused_computation.7 | convolution fusion | flops 3224371200 | bytes 16252928 | tf_op jit(solution)/shard_map/dot_general | solution.py:88
  15.9 0.0 reduce-scatter.2.cloned.1.call-update
  16.0 0.0 all-gather.3.cloned.1.call-start
  16.0 100.0 %reduce-scatter.2.cloned.1.call-done = f32[512,1536]{0,1:T(8,128)} async-done(((f32[2048,1536]{0,1:T(8,128)}), f32[512,1536]{0,1:T(8,128)}) %reduce-scatter.2.cloned.1.call-update) | async-done | bytes 3145744 | tf_op jit(solution)/shard_map/reduce_scatter | solution.py:87
  116.0 2.1 convert_element_type.20
  118.1 1.1 slice_bitcast_fusion
  119.1 1.5 collective-permute-start
  120.6 0.1 copy.36
  120.7 0.1 reduce
  120.9 0.1 convert_reduce_fusion.1
  121.0 0.1 convert_reduce_fusion
  121.1 0.5 fusion.7
  121.5 1.1 convolution_convert_fusion.1
  122.6 2.4 collective-permute-start.1
  125.0 0.8 slice.9
  125.9 0.0 all-gather.3.cloned.1.call-update
  125.9 21.4 %collective-permute-done = bf16[512,1,1024]{0,2,1:T(8,128)(2,1)} collective-permute-done((bf16[512,1,1024]{0,2,1:T(8,128)(2,1)}, bf16[512,1,1024]{0,2,1:T(8,128)(2,1)}, u32[]{:S(2)}, u32[]{:S(2)}) %collective-permute-start) | collective-permute-done | bytes 1048608 | tf_op jit(solution)/shard_map/ppermute | solution.py:18
  147.3 29.4 %copy_multiply_fusion = bf16[32,1024,512]{2,0,1:T(8,128)(2,1)} fusion(bf16[32,1024,512]{2,1,0:T(8,128)(2,1)} %param.11, bf16[1024,512]{1,0:T(8,128)(2,1)S(1)} %convolution_convert_fusion.1), kind=kLoop, calls=%fused_computation.6 | loop fusion | flops 16777216 | bytes 68157440 | tf_op jit(solution)/shard_map/mul | solution.py:99
  176.7 0.6 dynamic-slice
  177.3 1.5 copy.32
  178.8 2.6 broadcast_in_dim.8
  181.4 1.1 constant_dynamic-update-slice_fusion.3
  182.5 1.5 copy.33
  184.0 1.5 copy.34
  185.5 0.0 all-gather.3.cloned.1.call-done
  185.5 1.5 copy.38
  187.0 1.1 constant_dynamic-update-slice_fusion.2
  188.1 1.1 constant_dynamic-update-slice_fusion.1
  189.1 1.8 collective-permute-done.2
  191.0 1.5 copy.35
  192.5 1.1 constant_dynamic-update-slice_fusion
  193.5 92.4 %while.10 = (s32[]{:T(128)}, f32[4,2,32]{2,1,0:T(2,128)S(1)}, bf16[4,512,1024]{2,1,0:T(8,128)(2,1)}, bf16[512,1024]{1,0:T(8,128)(2,1)S(1)}, bf16[32,1024,512]{2,0,1:T(8,128)(2,1)}, /*index=5*/s32[]{:T(128)}) while((s32[]{:T(128)}, f32[4,2,32]{2,1,0:T(2,128)S(1)}, bf16[4,512,1024]{2,1,0:T(8,128)(2,1)}, bf16[512,1024]{1,0:T(8,128)(2,1)S(1)}, ...), condition=%wide.region_5.6_spmd, body=%wide.region_4.5_spmd.sunk | while | flops 1141899264 | bytes 44041800 | solution.py:69
  193.5 3.8 %convolution_convert_fusion.3 = bf16[1024,1024]{0,1:T(8,128)(2,1)} fusion(bf16[512,1024]{1,0:T(8,128)(2,1)S(1)} %get-tuple-element.109, bf16[4,512,1024]{2,1,0:T(8,128)(2,1)} %get-tuple-element.108, s32[]{:T(128)} %get-tuple-element.100), kind=kOutput, calls=%fused_computation.clone.1 | convolution fusion | flops 1074790400 | bytes 4194816 | tf_op jit(solution)/shard_map/while/body/eval_jaxpr/dot_general | solution.py:60
  197.3 4.8 %copy.41 = bf16[1024,2,512]{2,1,0:T(2,128)(2,1)S(1)} copy(bf16[1024,2,512]{0,2,1:T(8,128)(2,1)} %bitcast.38) | data formatting | bytes 4194304 | tf_op jit(solution)/shard_map/while/body/eval_jaxpr/reshape | solution.py:63
  202.2 14.4 %fusion.26 = f32[4,2,32]{2,1,0:T(2,128)S(1)} fusion(f32[4,2,32]{2,1,0:T(2,128)S(1)} %get-tuple-element.101, s32[]{:T(128)} %get-tuple-element.100, bf16[1024,2,512]{2,1,0:T(2,128)(2,1)S(1)} %copy.41, bf16[32,1024,512]{2,0,1:T(8,128)(2,1)} %get-tuple-element.110), kind=kOutput, calls=%fused_computation.2.clone.1 | convolution fusion | flops 67108864 | bytes 35652612 | tf_op jit(solution)/shard_map/while/body/eval_jaxpr/dot_general | solution.py:64
  216.6 3.8 %convolution_convert_fusion.3 = bf16[1024,1024]{0,1:T(8,128)(2,1)} fusion(bf16[512,1024]{1,0:T(8,128)(2,1)S(1)} %get-tuple-element.109, bf16[4,512,1024]{2,1,0:T(8,128)(2,1)} %get-tuple-element.108, s32[]{:T(128)} %get-tuple-element.100), kind=kOutput, calls=%fused_computation.clone.1 | convolution fusion | flops 1074790400 | bytes 4194816 | tf_op jit(solution)/shard_map/while/body/eval_jaxpr/dot_general | solution.py:60
  220.4 4.8 %copy.41 = bf16[1024,2,512]{2,1,0:T(2,128)(2,1)S(1)} copy(bf16[1024,2,512]{0,2,1:T(8,128)(2,1)} %bitcast.38) | data formatting | bytes 4194304 | tf_op jit(solution)/shard_map/while/body/eval_jaxpr/reshape | solution.py:63
  225.3 14.4 %fusion.26 = f32[4,2,32]{2,1,0:T(2,128)S(1)} fusion(f32[4,2,32]{2,1,0:T(2,128)S(1)} %get-tuple-element.101, s32[]{:T(128)} %get-tuple-element.100, bf16[1024,2,512]{2,1,0:T(2,128)(2,1)S(1)} %copy.41, bf16[32,1024,512]{2,0,1:T(8,128)(2,1)} %get-tuple-element.110), kind=kOutput, calls=%fused_computation.2.clone.1 | convolution fusion | flops 67108864 | bytes 35652612 | tf_op jit(solution)/shard_map/while/body/eval_jaxpr/dot_general | solution.py:64
  239.7 3.8 %convolution_convert_fusion.3 = bf16[1024,1024]{0,1:T(8,128)(2,1)} fusion(bf16[512,1024]{1,0:T(8,128)(2,1)S(1)} %get-tuple-element.109, bf16[4,512,1024]{2,1,0:T(8,128)(2,1)} %get-tuple-element.108, s32[]{:T(128)} %get-tuple-element.100), kind=kOutput, calls=%fused_computation.clone.1 | convolution fusion | flops 1074790400 | bytes 4194816 | tf_op jit(solution)/shard_map/while/body/eval_jaxpr/dot_general | solution.py:60
  243.5 4.8 %copy.41 = bf16[1024,2,512]{2,1,0:T(2,128)(2,1)S(1)} copy(bf16[1024,2,512]{0,2,1:T(8,128)(2,1)} %bitcast.38) | data formatting | bytes 4194304 | tf_op jit(solution)/shard_map/while/body/eval_jaxpr/reshape | solution.py:63
  248.3 14.4 %fusion.26 = f32[4,2,32]{2,1,0:T(2,128)S(1)} fusion(f32[4,2,32]{2,1,0:T(2,128)S(1)} %get-tuple-element.101, s32[]{:T(128)} %get-tuple-element.100, bf16[1024,2,512]{2,1,0:T(2,128)(2,1)S(1)} %copy.41, bf16[32,1024,512]{2,0,1:T(8,128)(2,1)} %get-tuple-element.110), kind=kOutput, calls=%fused_computation.2.clone.1 | convolution fusion | flops 67108864 | bytes 35652612 | tf_op jit(solution)/shard_map/while/body/eval_jaxpr/dot_general | solution.py:64
  262.8 3.8 %convolution_convert_fusion.3 = bf16[1024,1024]{0,1:T(8,128)(2,1)} fusion(bf16[512,1024]{1,0:T(8,128)(2,1)S(1)} %get-tuple-element.109, bf16[4,512,1024]{2,1,0:T(8,128)(2,1)} %get-tuple-element.108, s32[]{:T(128)} %get-tuple-element.100), kind=kOutput, calls=%fused_computation.clone.1 | convolution fusion | flops 1074790400 | bytes 4194816 | tf_op jit(solution)/shard_map/while/body/eval_jaxpr/dot_general | solution.py:60
  266.6 4.8 %copy.41 = bf16[1024,2,512]{2,1,0:T(2,128)(2,1)S(1)} copy(bf16[1024,2,512]{0,2,1:T(8,128)(2,1)} %bitcast.38) | data formatting | bytes 4194304 | tf_op jit(solution)/shard_map/while/body/eval_jaxpr/reshape | solution.py:63
  271.4 14.4 %fusion.26 = f32[4,2,32]{2,1,0:T(2,128)S(1)} fusion(f32[4,2,32]{2,1,0:T(2,128)S(1)} %get-tuple-element.101, s32[]{:T(128)} %get-tuple-element.100, bf16[1024,2,512]{2,1,0:T(2,128)(2,1)S(1)} %copy.41, bf16[32,1024,512]{2,0,1:T(8,128)(2,1)} %get-tuple-element.110), kind=kOutput, calls=%fused_computation.2.clone.1 | convolution fusion | flops 67108864 | bytes 35652612 | tf_op jit(solution)/shard_map/while/body/eval_jaxpr/dot_general | solution.py:64
  285.9 20.2 %all-reduce = f32[8,32]{1,0:T(8,128)S(1)} all-reduce(f32[8,32]{1,0:T(8,128)S(1)} %bitcast.39), channel_id=4, replica_groups=mesh['aux'=4,'cd'=4,'ab'=2] {'cd','ab'}, use_global_device_ids=true, to_apply=%region_6.7.clone | all-reduce | flops 256 | bytes 2048
  306.1 0.6 dynamic-slice_bitcast_fusion
  306.7 6.4 %psum.7 = f32[1,1,32]{2,1,0:T(1,128)} all-reduce(f32[1,1,32]{2,1,0:T(1,128)S(1)} %dynamic-slice_bitcast_fusion), channel_id=1, replica_groups=mesh['aux'=4,'cd'=4,'ab'=2] {'aux'}, use_global_device_ids=true, to_apply=%region_7.8 | all-reduce | flops 32 | bytes 256 | tf_op jit(solution)/shard_map/psum | solution.py:103
  (16 shorter events, 0.1 us)
Async XLA Ops:
  6.5 1.6 copy-start
  6.5 109.4 %reduce-scatter.2.cloned.1.call-start = ((), (), s32[]{:S(2)}) async-start(), calls=%async_computation.1 | async-start | bytes 15728640 | tf_op jit(solution)/shard_map/reduce_scatter | solution.py:87
  15.9 104.7 %copy-start.2 = (s32[16]{0:T(128)S(1)}, s32[16]{0:T(128)}, u32[]{:S(2)}) copy-start(s32[16]{0:T(128)} %param.12) | copy-start | bytes 196
  15.9 105.1 %copy-start.3 = (s32[16,16]{1,0:T(8,128)S(1)}, s32[16,16]{1,0:T(8,128)}, u32[]{:S(2)}) copy-start(s32[16,16]{1,0:T(8,128)} %param.13) | copy-start | bytes 3076
  16.0 169.5 %all-gather.3.cloned.1.call-start = ((), (), s32[]{:S(2)}) async-start(), calls=%async_computation.2 | async-start | bytes 1572864 | tf_op jit(solution)/shard_map/all_gather | solution.py:97
  119.1 28.2 %collective-permute-start = (bf16[512,1,1024]{0,2,1:T(8,128)(2,1)}, bf16[512,1,1024]{0,2,1:T(8,128)(2,1)}, u32[]{:S(2)}, u32[]{:S(2)}) collective-permute-start(bf16[512,1,1024]{0,2,1:T(8,128)(2,1)} %slice_bitcast_fusion), channel_id=1, source_target_pairs={{0,2},{2,4},{4,6},{6,0},{1,3},{3,5},{5,7},{7,1},{8,10},{10,12},{12... | collective-permute-start | bytes 3145736 | tf_op jit(solution)/shard_map/ppermute | solution.py:18
  122.6 61.3 %collective-permute-start.1 = (bf16[512,1,1024]{0,2,1:T(8,128)(2,1)}, bf16[512,1,1024]{0,2,1:T(8,128)(2,1)}, u32[]{:S(2)}, u32[]{:S(2)}) collective-permute-start(bf16[512,1,1024]{0,2,1:T(8,128)(2,1)} %slice_bitcast_fusion), channel_id=1, source_target_pairs={{0,6},{2,0},{4,2},{6,4},{1,7},{3,1},{5,3},{7,5},{8,14},{10,8},{12,... | collective-permute-start | bytes 3145736 | tf_op jit(solution)/shard_map/ppermute | solution.py:25
  125.9 50.8 %copy-start.4 = (u32[32]{0:T(128)S(1)}, u32[32]{0:T(128)}, u32[]{:S(2)}) copy-start(u32[32]{0:T(128)} %constant.61) | copy-start | bytes 388
  147.3 43.7 %collective-permute-start.2 = (bf16[512,1,1024]{0,2,1:T(8,128)(2,1)}, bf16[512,1,1024]{0,2,1:T(8,128)(2,1)}, u32[]{:S(2)}, u32[]{:S(2)}) collective-permute-start(bf16[512,1,1024]{0,2,1:T(8,128)(2,1)} %collective-permute-done), channel_id=1, source_target_pairs={{0,2},{2,4},{4,6},{6,0},{1,3},{3,5},{5,7},{7,1},{8,10},{10,12},{12... | collective-permute-start | bytes 3145736 | tf_op jit(solution)/shard_map/ppermute | solution.py:18
  285.9 27.2 %copy-start.1 = (bf16[512,2048]{1,0:T(8,128)(2,1)S(1)}, bf16[512,2048]{1,0:T(8,128)(2,1)}, u32[]{:S(2)}) copy-start(bf16[512,2048]{1,0:T(8,128)(2,1)} %param.10) | copy-start | bytes 6291460
Sparse Core Ops, SparseCore 0:
  16.1 99.8 reduce-scatter.1
  126.0 19.4 all-gather.2
